TPU v7x, 32 devices: a whole 2x2x4 slice. The times are simulated.
32 devices in a mesh: row: 8 (over z, x), col: 4 (over y, core).
Axes of the slice: x: 2, y: 2, z: 4, core: 2. Of those that a mesh axis runs over, the one named last changes fastest.
Arguments:
- tmatrix: bfloat16 [10656, 10656], P('row', 'col'), may hold values from -0.0625 to 0.0625
- panel: bfloat16 [10656, 2048], P('col', 'row'), may hold values from -6 to 6
- contrast: float32 [3, 144, 288], replicated, may hold values from -1.5 to 1.5
Outputs:
- excitation: bfloat16 [10656, 2048], P('col', 'row')
All inputs are finite; a program needn't handle non-finite values.
Results may differ from a plain program's by a relative error of at most 0.006.
Values may be sent and summed in bfloat16 or wider, within the bound.
No kernel may reach another device: no remote copies, remote signals or barrier semaphores. Data moves between devices by JAX's collectives and lax.ppermute only.
A program may use at most 192 MiB of HBM per device.

v0:
```python
import jax
import jax.numpy as jnp
import numpy as np
from jax import lax
from jax.sharding import PartitionSpec as P

LDEG = 72
ITERS = 2


def angular_tables(degree):
    lat_count = 2 * degree
    lon_count = 4 * degree
    freq_count = 2 * degree + 1
    colatitude = (np.arange(lat_count) + 0.5) * np.pi / lat_count
    cos_col = np.cos(colatitude)
    sin_col = np.sin(colatitude)
    legendre = np.zeros((freq_count, degree, lat_count))
    diagonal_term = np.full(lat_count, np.sqrt(0.5))
    for order_m in range(degree + 1):
        if order_m > 0:
            diagonal_term = (
                diagonal_term * np.sqrt((2.0 * order_m + 1.0) / (2.0 * order_m)) * sin_col
            )
        earlier = np.zeros(lat_count)
        latest = diagonal_term
        for degree_l in range(order_m, degree + 1):
            if degree_l == order_m:
                current = diagonal_term
            elif degree_l == order_m + 1:
                current = np.sqrt(2.0 * order_m + 3.0) * cos_col * diagonal_term
            else:
                factor_a = np.sqrt((4.0 * degree_l**2 - 1.0) / (degree_l**2 - order_m**2))
                factor_b = np.sqrt(
                    ((degree_l - 1.0) ** 2 - order_m**2) / (4.0 * (degree_l - 1.0) ** 2 - 1.0)
                )
                current = factor_a * (cos_col * latest - factor_b * earlier)
            if degree_l > order_m:
                earlier, latest = (latest, current)
            if degree_l >= 1:
                legendre[order_m, degree_l - 1] = current
                if order_m >= 1:
                    legendre[degree + order_m, degree_l - 1] = current
    longitude = 2.0 * np.pi * np.arange(lon_count) / lon_count
    fourier = np.zeros((freq_count, lon_count))
    fourier[0] = 1.0 / np.sqrt(2.0 * np.pi)
    for order_m in range(1, degree + 1):
        fourier[order_m] = np.cos(order_m * longitude) / np.sqrt(np.pi)
        fourier[degree + order_m] = np.sin(order_m * longitude) / np.sqrt(np.pi)
    weight = sin_col * (np.pi / lat_count) * (2.0 * np.pi / lon_count)
    return (legendre, fourier, weight)


def level_skips(degree):
    skips = []
    for freq_index in range(2 * degree + 1):
        order_m = freq_index if freq_index <= degree else freq_index - degree
        skips.append(max(order_m - 1, 0))
    return skips


def spread_levels(halves, degree):
    columns = halves.shape[2]
    pieces = []
    start = 0
    for skip in level_skips(degree):
        count = degree - skip
        if skip > 0:
            pieces.append(jnp.zeros((2, skip, columns), halves.dtype))
        pieces.append(halves[:, start : start + count, :])
        start = start + count
    return jnp.concatenate(pieces, axis=1).reshape(2, 2 * degree + 1, degree, columns)


def pick_levels(projected, degree):
    pieces = []
    for freq_index, skip in enumerate(level_skips(degree)):
        pieces.append(projected[:, freq_index, skip:, :])
    return jnp.concatenate(pieces, axis=1)


def contrast_apply(coefficients, contrast, degree):
    legendre, fourier, weight = angular_tables(degree)
    legendre_wide = jnp.asarray(legendre, jnp.float32)
    legendre_narrow = jnp.asarray(legendre, jnp.bfloat16)
    fourier = jnp.asarray(fourier, jnp.float32)
    weight = jnp.asarray(weight, jnp.float32)
    columns = coefficients.shape[1]
    halves = coefficients.astype(jnp.bfloat16).reshape(2, -1, columns)
    padded = spread_levels(halves, degree)
    triple = lax.Precision.HIGH
    latitude = jnp.einsum(
        "qlt,cqlk->cktq", legendre_narrow, padded, preferred_element_type=jnp.float32
    )
    surface = jnp.einsum(
        "cktq,qp->cktp", latitude, fourier, precision=triple, preferred_element_type=jnp.float32
    )
    polar = contrast[0] * surface[0] + contrast[1] * surface[1]
    azimuth = contrast[1] * surface[0] + contrast[2] * surface[1]
    weighted = jnp.stack([polar, azimuth]) * weight[:, None]
    spectrum = jnp.einsum(
        "cktp,qp->cktq", weighted, fourier, precision=triple, preferred_element_type=jnp.float32
    )
    projected = jnp.einsum(
        "qlt,cktq->cqlk",
        legendre_wide,
        spectrum,
        precision=triple,
        preferred_element_type=jnp.float32,
    )
    picked = pick_levels(projected, degree)
    return picked.reshape(-1, columns).astype(jnp.bfloat16)


def body(tmatrix, panel, contrast):
    row_count = lax.axis_size("row")
    col_count = lax.axis_size("col")
    per_device = panel.shape[1] // col_count
    local_rows = tmatrix.shape[0]
    current = panel
    for iteration in range(ITERS):
        partial_value = jnp.dot(
            tmatrix,
            lax.all_gather(current, "row", axis=1, tiled=True),
            preferred_element_type=jnp.float32,
        )
        grouped = partial_value.reshape(local_rows, row_count, col_count, per_device)
        summed = lax.psum_scatter(
            grouped.astype(jnp.bfloat16), "col", scatter_dimension=2, tiled=True
        )
        arrived = lax.all_to_all(summed, "row", split_axis=1, concat_axis=0, tiled=True)
        coupled = contrast_apply(
            arrived.reshape(arrived.shape[0], arrived.shape[3]), contrast, LDEG
        )
        full_rows = coupled.shape[0]
        returned = lax.all_to_all(
            coupled.reshape(col_count, full_rows // col_count, 1, per_device),
            "col",
            split_axis=0,
            concat_axis=2,
            tiled=True,
        )
        returned = returned.reshape(full_rows // col_count, col_count * per_device)
        current = (panel.astype(jnp.float32) + returned.astype(jnp.float32)).astype(jnp.bfloat16)
    return current


def solution(mesh):
    placed = (P("row", "col"), P("col", "row"), P())
    return jax.shard_map(
        body, mesh=mesh, in_specs=placed, out_specs=P("col", "row"), check_vma=False
    )
```

profile of v0, /device:TPU:0, one launch (start us, length us, event | category | flops | bytes accessed | tf_op | source)
XLA Modules:
  0.0 1476.1 jit_solution(9738215199244537752)
XLA Ops:
  7.3 160.5 %all-gather.3.cloned.1.call-done = bf16[2664,2048]{1,0:T(8,128)(2,1)} async-done(((bf16[2664,256]{1,0:T(8,128)(2,1)}), bf16[2664,2048]{1,0:T(8,128)(2,1)}) %all-gather.3.cloned.1.call-update) | async-done | bytes 10911760 | tf_op jit(solution)/shard_map/all_gather | solution.py:124
  167.9 21.4 %convolution_convert_fusion.1 = bf16[1332,2048]{1,0:T(8,128)(2,1)} fusion(bf16[1332,2664]{1,0:T(8,128)(2,1)} %param.11, bf16[2664,2048]{1,0:T(8,128)(2,1)} %all-gather.3.cloned.1.call-done), kind=kOutput, calls=%fused_computation.21 | convolution fusion | flops 14537170944 | bytes 23464512 | tf_op jit(solution)/shard_map/dot_general | solution.py:122
  189.3 8.2 copy.53
  198.7 108.2 %all-reduce.5.cloned.1.call-done = bf16[1332,8,4,64]{0,3,2,1:T(8,128)(2,1)} async-done(((bf16[1332,8,4,64]{0,3,2,1:T(8,128)(2,1)}), bf16[1332,8,4,64]{0,3,2,1:T(8,128)(2,1)}) %all-reduce.5.cloned.1.call-update) | async-done | bytes 5455888
  306.9 3.2 constant_dynamic-slice_fusion.1
  310.1 5.5 all-to-all-start
  316.4 33.1 %all-to-all-done = bf16[1332,8,1,64]{0,3,2,1:T(8,128)(2,1)S(1)} async-done(((bf16[1332,8,1,64]{0,3,2,1:T(8,128)(2,1)}), bf16[1332,8,1,64]{0,3,2,1:T(8,128)(2,1)S(1)}, u32[]{:S(2)}, u32[]{:S(2)}) %all-to-all-start) | async-done | bytes 1364000 | tf_op jit(solution)/shard_map/all_to_all | solution.py:131
  350.3 1.8 reshape_reshape.6
  407.0 5.4 concatenate.24
  426.7 55.6 %concatenate.23 = bf16[2,9417,64]{1,0,2:T(2,128)(2,1)} concatenate(bf16[2,144,64]{1,0,2:T(2,128)(2,1)S(1)} %slice.2639, bf16[2,1,64]{1,0,2:T(2,128)(2,1)S(1)} %broadcast.223, bf16[2,71,64]{1,0,2:T(2,128)(2,1)} %get-tuple-element.454, bf16[2,2,64]{1,0,2:T(2,128)(2,1)S(1)} %broadcast.224, bf16[2,70,64]{1,0,2:T(2,128)(2,1)} %get-tuple-element.452, ...), dimensions={1} | concatenate | bytes 4821504
  482.3 4.3 pad_maximum_fusion
  486.6 9.2 reshape.61
  495.8 13.2 convolution_bitcast_fusion.1
  509.0 39.7 %fusion.8 = f32[2,64,144,288]{3,2,1,0:T(8,128)} fusion(f32[145,288,1,1]{1,0,3,2:T(8,128)S(1)} %copy-done.6, f32[2,64,144,145]{2,1,0,3:T(8,128)} %convolution_bitcast_fusion.1), kind=kOutput, calls=%fused_computation.10 | convolution fusion | flops 4618321920 | bytes 32091264 | tf_op jit(solution)/shard_map/cktq,qp->cktp/dot_general | solution.py:95
  548.7 15.1 %multiply_add_fusion.3 = (f32[1,64,144,288]{3,2,1,0:T(8,128)S(1)}, f32[1,64,144,288]{3,2,1,0:T(8,128)}) fusion(f32[2,64,144,288]{3,2,1,0:T(8,128)} %fusion.8, f32[144,288]{1,0:T(8,128)} %get-tuple-element.457, f32[144,288]{1,0:T(8,128)S(1)} %get-tuple-element.455, f32[144,288]{1,0:T(8,128)S(1)} %get-tuple-element.456), kind=kLoop, calls=%fused_computation.17 | loop fusion | flops 15925248 | bytes 42964992 | tf_op jit(solution)/shard_map/add | solution.py:98
  563.9 20.4 %fusion = f32[2,64,144,145]{3,2,1,0:T(8,128)} fusion(f32[145,288,1,1]{1,0,3,2:T(8,128)} %constant.19, f32[1,64,144,288]{3,2,1,0:T(8,128)} %get-tuple-element.8, f32[1,64,144,288]{3,2,1,0:T(8,128)S(1)} %get-tuple-element.7, f32[144]{0:T(256)S(1)} %copy-done.84), kind=kOutput, calls=%fused_computation.1 | convolution fusion | flops 4628938752 | bytes 32091840 | tf_op jit(solution)/shard_map/cktp,qp->cktq/dot_general | solution.py:101
  584.3 22.2 %copy.58 = f32[2,64,144,145]{2,1,0,3:T(8,128)} copy(f32[2,64,144,145]{3,2,1,0:T(8,128)} %fusion) | data formatting | bytes 21381120 | tf_op jit(solution)/shard_map/cktp,qp->cktq/dot_general | solution.py:101
  606.4 14.8 %convert_bitcast_fusion.1 = bf16[2,145,72,64]{2,3,0,1:T(8,128)(2,1)} fusion(f32[2,64,144,145]{2,1,0,3:T(8,128)} %copy.58, f32[145,72,144,1]{2,1,3,0:T(8,128)} %constant.20), kind=kOutput, calls=%fused_computation.26 | convolution fusion | flops 1155916800 | bytes 19376640 | tf_op jit(solution)/shard_map/qlt,cktq->cqlk/dot_general | solution.py:104
  669.7 1.5 slice_bitcast_fusion.210
  681.6 1.5 slice_bitcast_fusion.218
  683.1 1.5 slice_bitcast_fusion.148
  701.0 1.5 slice_bitcast_fusion.160
  708.5 5.7 concatenate.17
  717.9 3.5 all-to-all-start.1
  721.5 1.8 copy.52
  723.3 16.0 %all-to-all-done.1 = bf16[4,2664,1,64]{1,3,2,0:T(8,128)(2,1)S(1)} async-done(((bf16[4,2664,1,64]{1,3,2,0:T(8,128)(2,1)}), bf16[4,2664,1,64]{1,3,2,0:T(8,128)(2,1)S(1)}, u32[]{:S(2)}, u32[]{:S(2)}) %all-to-all-start.1) | async-done | bytes 1364000 | tf_op jit(solution)/shard_map/all_to_all | solution.py:136
  741.0 155.1 %all-gather.5.cloned.1.call-done = bf16[2664,2048]{0,1:T(8,128)(2,1)} async-done(((bf16[2664,256]{0,1:T(8,128)(2,1)}), bf16[2664,2048]{0,1:T(8,128)(2,1)}) %all-gather.5.cloned.1.call-update) | async-done | bytes 10911760 | tf_op jit(solution)/shard_map/all_gather | solution.py:124
  896.1 21.5 %fusion.12 = bf16[1332,2048]{1,0:T(8,128)(2,1)} fusion(bf16[2664,2048]{0,1:T(8,128)(2,1)} %all-gather.5.cloned.1.call-done, bf16[1332,2664]{1,0:T(8,128)(2,1)} %param.11), kind=kOutput, calls=%fused_computation.22 | convolution fusion | flops 14537170944 | bytes 23464512 | tf_op jit(solution)/shard_map/dot_general | solution.py:122
  917.6 8.2 copy.63
  925.8 109.4 %all-reduce.7.cloned.1.call-done = bf16[1332,8,4,64]{0,3,2,1:T(8,128)(2,1)} async-done(((bf16[1332,8,4,64]{0,3,2,1:T(8,128)(2,1)}), bf16[1332,8,4,64]{0,3,2,1:T(8,128)(2,1)}) %all-reduce.7.cloned.1.call-update) | async-done | bytes 5455888
  1035.2 2.1 constant_dynamic-slice_fusion
  1037.3 39.5 %all_to_all.48 = bf16[1332,8,1,64]{0,3,2,1:T(8,128)(2,1)S(1)} all-to-all(bf16[1332,8,1,64]{0,3,2,1:T(8,128)(2,1)S(1)} %constant_dynamic-slice_fusion), channel_id=1, replica_groups=mesh['row'=8,'col'=4] {'row'}, dimensions={1} | all-to-all | bytes 2727936 | tf_op jit(solution)/shard_map/all_to_all | solution.py:131
  1077.6 1.8 reshape_reshape.7
  1133.9 4.7 concatenate.21
  1139.0 59.3 %concatenate.20 = bf16[2,9417,64]{1,0,2:T(2,128)(2,1)} concatenate(bf16[2,144,64]{1,0,2:T(2,128)(2,1)S(1)} %slice.2929, bf16[2,1,64]{1,0,2:T(2,128)(2,1)S(1)} %copy-done.9, bf16[2,71,64]{1,0,2:T(2,128)(2,1)} %get-tuple-element.342, bf16[2,2,64]{1,0,2:T(2,128)(2,1)S(1)} %copy-done.11, bf16[2,70,64]{1,0,2:T(2,128)(2,1)} %get-tuple-element.340, bf16[2,3,64]{1,0,2:T(2,128)(2,1)S(1)} %copy-done.13, ...), dimensions={1} | concatenate | bytes 4821504
  1198.3 4.3 pad_maximum_fusion.1
  1202.6 9.2 reshape.62
  1211.8 13.2 convolution_bitcast_fusion
  1225.0 39.5 %fusion.6 = f32[2,64,144,288]{3,2,1,0:T(8,128)} fusion(f32[145,288,1,1]{1,0,3,2:T(8,128)S(1)} %copy-done.7, f32[2,64,144,145]{2,1,0,3:T(8,128)} %convolution_bitcast_fusion), kind=kOutput, calls=%fused_computation.8 | convolution fusion | flops 4618321920 | bytes 32091264 | tf_op jit(solution)/shard_map/cktq,qp->cktp/dot_general | solution.py:95
  1264.6 15.1 %multiply_add_fusion.1 = (f32[1,64,144,288]{3,2,1,0:T(8,128)S(1)}, f32[1,64,144,288]{3,2,1,0:T(8,128)}) fusion(f32[2,64,144,288]{3,2,1,0:T(8,128)} %fusion.6, f32[144,288]{1,0:T(8,128)} %get-tuple-element.457, f32[144,288]{1,0:T(8,128)S(1)} %copy-done.3, f32[144,288]{1,0:T(8,128)S(1)} %copy-done.5), kind=kLoop, calls=%fused_computation.13 | loop fusion | flops 15925248 | bytes 42964992 | tf_op jit(solution)/shard_map/add | solution.py:98
  1279.7 20.4 %fusion.3 = f32[2,64,144,145]{3,2,1,0:T(8,128)} fusion(f32[145,288,1,1]{1,0,3,2:T(8,128)} %constant.19, f32[1,64,144,288]{3,2,1,0:T(8,128)} %get-tuple-element.6, f32[1,64,144,288]{3,2,1,0:T(8,128)S(1)} %get-tuple-element.5, f32[144]{0:T(256)S(1)} %copy-done.85), kind=kOutput, calls=%fused_computation.5 | convolution fusion | flops 4628938752 | bytes 32091840 | tf_op jit(solution)/shard_map/cktp,qp->cktq/dot_general | solution.py:101
  1300.1 22.2 %copy.68 = f32[2,64,144,145]{2,1,0,3:T(8,128)} copy(f32[2,64,144,145]{3,2,1,0:T(8,128)} %fusion.3) | data formatting | bytes 21381120 | tf_op jit(solution)/shard_map/cktp,qp->cktq/dot_general | solution.py:101
  1322.3 14.9 %convert_bitcast_fusion = bf16[2,145,72,64]{2,3,0,1:T(8,128)(2,1)} fusion(f32[2,64,144,145]{2,1,0,3:T(8,128)} %copy.68, f32[145,72,144,1]{2,1,3,0:T(8,128)} %constant.20), kind=kOutput, calls=%fused_computation.25 | convolution fusion | flops 1155916800 | bytes 19376640 | tf_op jit(solution)/shard_map/qlt,cktq->cqlk/dot_general | solution.py:104
  1391.8 1.5 slice_bitcast_fusion.53
  1406.7 1.5 slice_bitcast_fusion.63
  1438.4 5.7 concatenate.19
  1446.7 20.5 %all_to_all.49 = bf16[4,2664,1,64]{1,3,2,0:T(8,128)(2,1)S(1)} all-to-all(bf16[4,2664,1,64]{1,3,2,0:T(8,128)(2,1)S(1)} %copy.72), channel_id=1, replica_groups=mesh['row'=8,'col'=4] {'col'}, dimensions={0} | all-to-all | bytes 2727936 | tf_op jit(solution)/shard_map/all_to_all | solution.py:136
  1467.6 1.5 copy.73
  (594 shorter events, 313.9 us)
Async XLA Ops:
  6.5 161.3 %all-gather.3.cloned.1.call-start = ((), (), s32[]{:S(2)}) async-start(), calls=%async_computation.4 | async-start | bytes 12275712 | tf_op jit(solution)/shard_map/all_gather | solution.py:124
  7.3 299.7 %all-reduce.5.cloned.1.call-start = ((), (), s32[]{:S(2)}) async-start(), calls=%async_computation.6 | async-start | bytes 11534336
  197.5 118.1 %copy-start.82 = (f32[3,144,288]{2,1,0:T(8,128)S(1)}, f32[3,144,288]{2,1,0:T(8,128)}, u32[]{:S(2)}) copy-start(f32[3,144,288]{2,1,0:T(8,128)} %param.13) | copy-start | bytes 1492996
  310.1 39.3 %all-to-all-start = ((bf16[1332,8,1,64]{0,3,2,1:T(8,128)(2,1)}), bf16[1332,8,1,64]{0,3,2,1:T(8,128)(2,1)S(1)}, u32[]{:S(2)}, u32[]{:S(2)}) async-start(bf16[1332,8,1,64]{0,3,2,1:T(8,128)(2,1)} %constant_dynamic-slice_fusion.1), calls=%async_computation | async-start | bytes 2883584 | tf_op jit(solution)/shard_map/all_to_all | solution.py:131
  316.4 232.3 %copy-start.2 = (f32[144,288]{1,0:T(8,128)}, f32[144,288]{1,0:T(8,128)S(1)}, u32[]{:S(2)}) copy-start(f32[144,288]{1,0:T(8,128)S(1)} %get-tuple-element.455) | copy-start | bytes 497668
  316.4 232.3 %copy-start.4 = (f32[144,288]{1,0:T(8,128)}, f32[144,288]{1,0:T(8,128)S(1)}, u32[]{:S(2)}) copy-start(f32[144,288]{1,0:T(8,128)S(1)} %get-tuple-element.456) | copy-start | bytes 497668
  412.4 69.9 %copy-start.8 = (bf16[2,1,64]{1,0,2:T(2,128)(2,1)}, bf16[2,1,64]{1,0,2:T(2,128)(2,1)S(1)}, u32[]{:S(2)}) copy-start(bf16[2,1,64]{1,0,2:T(2,128)(2,1)S(1)} %broadcast.223) | copy-start | bytes 772
  412.4 69.9 %copy-start.10 = (bf16[2,2,64]{1,0,2:T(2,128)(2,1)}, bf16[2,2,64]{1,0,2:T(2,128)(2,1)S(1)}, u32[]{:S(2)}) copy-start(bf16[2,2,64]{1,0,2:T(2,128)(2,1)S(1)} %broadcast.224) | copy-start | bytes 1540
  412.5 69.8 %copy-start.12 = (bf16[2,3,64]{1,0,2:T(2,128)(2,1)}, bf16[2,3,64]{1,0,2:T(2,128)(2,1)S(1)}, u32[]{:S(2)}) copy-start(bf16[2,3,64]{1,0,2:T(2,128)(2,1)S(1)} %broadcast.225) | copy-start | bytes 2308
  717.9 21.5 %all-to-all-start.1 = ((bf16[4,2664,1,64]{1,3,2,0:T(8,128)(2,1)}), bf16[4,2664,1,64]{1,3,2,0:T(8,128)(2,1)S(1)}, u32[]{:S(2)}, u32[]{:S(2)}) async-start(bf16[4,2664,1,64]{1,3,2,0:T(8,128)(2,1)} %copy.62), calls=%async_computation.1 | async-start | bytes 2752512 | tf_op jit(solution)/shard_map/all_to_all | solution.py:136
  721.4 174.7 %all-gather.5.cloned.1.call-start = ((), (), s32[]{:S(2)}) async-start(), calls=%async_computation.5 | async-start | bytes 12386304 | tf_op jit(solution)/shard_map/all_gather | solution.py:124
  740.9 294.3 %all-reduce.7.cloned.1.call-start = ((), (), s32[]{:S(2)}) async-start(), calls=%async_computation.7 | async-start | bytes 11534336
  1085.8 52.9 %copy-start.11 = (bf16[2,2,64]{1,0,2:T(2,128)(2,1)S(1)}, bf16[2,2,64]{1,0,2:T(2,128)(2,1)}, u32[]{:S(2)}) copy-start(bf16[2,2,64]{1,0,2:T(2,128)(2,1)} %copy-done.10) | copy-start | bytes 1540
  1085.8 52.9 %copy-start.13 = (bf16[2,3,64]{1,0,2:T(2,128)(2,1)S(1)}, bf16[2,3,64]{1,0,2:T(2,128)(2,1)}, u32[]{:S(2)}) copy-start(bf16[2,3,64]{1,0,2:T(2,128)(2,1)} %copy-done.12) | copy-start | bytes 2308
  1085.8 52.9 %copy-start.15 = (bf16[2,4,64]{1,0,2:T(2,128)(2,1)S(1)}, bf16[2,4,64]{1,0,2:T(2,128)(2,1)}, u32[]{:S(2)}) copy-start(bf16[2,4,64]{1,0,2:T(2,128)(2,1)} %copy-done.14) | copy-start | bytes 3076
  1085.8 52.9 %copy-start.17 = (bf16[2,5,64]{1,0,2:T(2,128)(2,1)S(1)}, bf16[2,5,64]{1,0,2:T(2,128)(2,1)}, u32[]{:S(2)}) copy-start(bf16[2,5,64]{1,0,2:T(2,128)(2,1)} %copy-done.16) | copy-start | bytes 3844
  1085.8 52.9 %copy-start.19 = (bf16[2,6,64]{1,0,2:T(2,128)(2,1)S(1)}, bf16[2,6,64]{1,0,2:T(2,128)(2,1)}, u32[]{:S(2)}) copy-start(bf16[2,6,64]{1,0,2:T(2,128)(2,1)} %copy-done.18) | copy-start | bytes 4612
  1085.8 52.9 %copy-start.21 = (bf16[2,7,64]{1,0,2:T(2,128)(2,1)S(1)}, bf16[2,7,64]{1,0,2:T(2,128)(2,1)}, u32[]{:S(2)}) copy-start(bf16[2,7,64]{1,0,2:T(2,128)(2,1)} %copy-done.20) | copy-start | bytes 5380
  1085.8 52.9 %copy-start.23 = (bf16[2,8,64]{1,0,2:T(2,128)(2,1)S(1)}, bf16[2,8,64]{1,0,2:T(2,128)(2,1)}, u32[]{:S(2)}) copy-start(bf16[2,8,64]{1,0,2:T(2,128)(2,1)} %copy-done.22) | copy-start | bytes 6148
  1085.8 52.9 %copy-start.25 = (bf16[2,9,64]{1,0,2:T(2,128)(2,1)S(1)}, bf16[2,9,64]{1,0,2:T(2,128)(2,1)}, u32[]{:S(2)}) copy-start(bf16[2,9,64]{1,0,2:T(2,128)(2,1)} %copy-done.24) | copy-start | bytes 6916
  1085.8 52.9 %copy-start.27 = (bf16[2,10,64]{1,0,2:T(2,128)(2,1)S(1)}, bf16[2,10,64]{1,0,2:T(2,128)(2,1)}, u32[]{:S(2)}) copy-start(bf16[2,10,64]{1,0,2:T(2,128)(2,1)} %copy-done.26) | copy-start | bytes 7684
  1085.8 52.9 %copy-start.29 = (bf16[2,11,64]{1,0,2:T(2,128)(2,1)S(1)}, bf16[2,11,64]{1,0,2:T(2,128)(2,1)}, u32[]{:S(2)}) copy-start(bf16[2,11,64]{1,0,2:T(2,128)(2,1)} %copy-done.28) | copy-start | bytes 8452
  1085.9 52.9 %copy-start.31 = (bf16[2,12,64]{1,0,2:T(2,128)(2,1)S(1)}, bf16[2,12,64]{1,0,2:T(2,128)(2,1)}, u32[]{:S(2)}) copy-start(bf16[2,12,64]{1,0,2:T(2,128)(2,1)} %copy-done.30) | copy-start | bytes 9220
  1085.9 52.9 %copy-start.33 = (bf16[2,13,64]{1,0,2:T(2,128)(2,1)S(1)}, bf16[2,13,64]{1,0,2:T(2,128)(2,1)}, u32[]{:S(2)}) copy-start(bf16[2,13,64]{1,0,2:T(2,128)(2,1)} %copy-done.32) | copy-start | bytes 9988
  1085.9 52.9 %copy-start.35 = (bf16[2,14,64]{1,0,2:T(2,128)(2,1)S(1)}, bf16[2,14,64]{1,0,2:T(2,128)(2,1)}, u32[]{:S(2)}) copy-start(bf16[2,14,64]{1,0,2:T(2,128)(2,1)} %copy-done.34) | copy-start | bytes 10756
  1085.9 52.9 %copy-start.37 = (bf16[2,15,64]{1,0,2:T(2,128)(2,1)S(1)}, bf16[2,15,64]{1,0,2:T(2,128)(2,1)}, u32[]{:S(2)}) copy-start(bf16[2,15,64]{1,0,2:T(2,128)(2,1)} %copy-done.36) | copy-start | bytes 11524
  1085.9 52.9 %copy-start.39 = (bf16[2,16,64]{1,0,2:T(2,128)(2,1)S(1)}, bf16[2,16,64]{1,0,2:T(2,128)(2,1)}, u32[]{:S(2)}) copy-start(bf16[2,16,64]{1,0,2:T(2,128)(2,1)} %copy-done.38) | copy-start | bytes 12292
  1085.9 52.9 %copy-start.41 = (bf16[2,17,64]{1,0,2:T(2,128)(2,1)S(1)}, bf16[2,17,64]{1,0,2:T(2,128)(2,1)}, u32[]{:S(2)}) copy-start(bf16[2,17,64]{1,0,2:T(2,128)(2,1)} %copy-done.40) | copy-start | bytes 13060
  1085.9 52.9 %copy-start.43 = (bf16[2,18,64]{1,0,2:T(2,128)(2,1)S(1)}, bf16[2,18,64]{1,0,2:T(2,128)(2,1)}, u32[]{:S(2)}) copy-start(bf16[2,18,64]{1,0,2:T(2,128)(2,1)} %copy-done.42) | copy-start | bytes 13828
  1085.9 52.9 %copy-start.45 = (bf16[2,19,64]{1,0,2:T(2,128)(2,1)S(1)}, bf16[2,19,64]{1,0,2:T(2,128)(2,1)}, u32[]{:S(2)}) copy-start(bf16[2,19,64]{1,0,2:T(2,128)(2,1)} %copy-done.44) | copy-start | bytes 14596
  1085.9 52.9 %copy-start.47 = (bf16[2,20,64]{1,0,2:T(2,128)(2,1)S(1)}, bf16[2,20,64]{1,0,2:T(2,128)(2,1)}, u32[]{:S(2)}) copy-start(bf16[2,20,64]{1,0,2:T(2,128)(2,1)} %copy-done.46) | copy-start | bytes 15364
  1086.0 52.9 %copy-start.49 = (bf16[2,21,64]{1,0,2:T(2,128)(2,1)S(1)}, bf16[2,21,64]{1,0,2:T(2,128)(2,1)}, u32[]{:S(2)}) copy-start(bf16[2,21,64]{1,0,2:T(2,128)(2,1)} %copy-done.48) | copy-start | bytes 16132
  1086.0 52.9 %copy-start.51 = (bf16[2,22,64]{1,0,2:T(2,128)(2,1)S(1)}, bf16[2,22,64]{1,0,2:T(2,128)(2,1)}, u32[]{:S(2)}) copy-start(bf16[2,22,64]{1,0,2:T(2,128)(2,1)} %copy-done.50) | copy-start | bytes 16900
  1086.0 52.9 %copy-start.53 = (bf16[2,23,64]{1,0,2:T(2,128)(2,1)S(1)}, bf16[2,23,64]{1,0,2:T(2,128)(2,1)}, u32[]{:S(2)}) copy-start(bf16[2,23,64]{1,0,2:T(2,128)(2,1)} %copy-done.52) | copy-start | bytes 17668
  1086.0 52.9 %copy-start.55 = (bf16[2,24,64]{1,0,2:T(2,128)(2,1)S(1)}, bf16[2,24,64]{1,0,2:T(2,128)(2,1)}, u32[]{:S(2)}) copy-start(bf16[2,24,64]{1,0,2:T(2,128)(2,1)} %copy-done.54) | copy-start | bytes 18436
  1086.0 52.9 %copy-start.57 = (bf16[2,25,64]{1,0,2:T(2,128)(2,1)S(1)}, bf16[2,25,64]{1,0,2:T(2,128)(2,1)}, u32[]{:S(2)}) copy-start(bf16[2,25,64]{1,0,2:T(2,128)(2,1)} %copy-done.56) | copy-start | bytes 19204
  1086.0 52.9 %copy-start.59 = (bf16[2,26,64]{1,0,2:T(2,128)(2,1)S(1)}, bf16[2,26,64]{1,0,2:T(2,128)(2,1)}, u32[]{:S(2)}) copy-start(bf16[2,26,64]{1,0,2:T(2,128)(2,1)} %copy-done.58) | copy-start | bytes 19972
  1086.0 52.9 %copy-start.61 = (bf16[2,27,64]{1,0,2:T(2,128)(2,1)S(1)}, bf16[2,27,64]{1,0,2:T(2,128)(2,1)}, u32[]{:S(2)}) copy-start(bf16[2,27,64]{1,0,2:T(2,128)(2,1)} %copy-done.60) | copy-start | bytes 20740
  1086.0 52.9 %copy-start.63 = (bf16[2,28,64]{1,0,2:T(2,128)(2,1)S(1)}, bf16[2,28,64]{1,0,2:T(2,128)(2,1)}, u32[]{:S(2)}) copy-start(bf16[2,28,64]{1,0,2:T(2,128)(2,1)} %copy-done.62) | copy-start | bytes 21508
  1086.0 52.9 %copy-start.65 = (bf16[2,29,64]{1,0,2:T(2,128)(2,1)S(1)}, bf16[2,29,64]{1,0,2:T(2,128)(2,1)}, u32[]{:S(2)}) copy-start(bf16[2,29,64]{1,0,2:T(2,128)(2,1)} %copy-done.64) | copy-start | bytes 22276
  1086.0 52.9 %copy-start.67 = (bf16[2,30,64]{1,0,2:T(2,128)(2,1)S(1)}, bf16[2,30,64]{1,0,2:T(2,128)(2,1)}, u32[]{:S(2)}) copy-start(bf16[2,30,64]{1,0,2:T(2,128)(2,1)} %copy-done.66) | copy-start | bytes 23044
  1086.0 52.9 %copy-start.69 = (bf16[2,31,64]{1,0,2:T(2,128)(2,1)S(1)}, bf16[2,31,64]{1,0,2:T(2,128)(2,1)}, u32[]{:S(2)}) copy-start(bf16[2,31,64]{1,0,2:T(2,128)(2,1)} %copy-done.68) | copy-start | bytes 23812
  1086.1 52.9 %copy-start.71 = (bf16[2,32,64]{1,0,2:T(2,128)(2,1)S(1)}, bf16[2,32,64]{1,0,2:T(2,128)(2,1)}, u32[]{:S(2)}) copy-start(bf16[2,32,64]{1,0,2:T(2,128)(2,1)} %copy-done.70) | copy-start | bytes 24580
  1086.1 52.9 %copy-start.73 = (bf16[2,33,64]{1,0,2:T(2,128)(2,1)S(1)}, bf16[2,33,64]{1,0,2:T(2,128)(2,1)}, u32[]{:S(2)}) copy-start(bf16[2,33,64]{1,0,2:T(2,128)(2,1)} %copy-done.72) | copy-start | bytes 25348
  1086.1 52.9 %copy-start.75 = (bf16[2,34,64]{1,0,2:T(2,128)(2,1)S(1)}, bf16[2,34,64]{1,0,2:T(2,128)(2,1)}, u32[]{:S(2)}) copy-start(bf16[2,34,64]{1,0,2:T(2,128)(2,1)} %copy-done.74) | copy-start | bytes 26116
  1086.1 52.9 %copy-start.77 = (bf16[2,35,64]{1,0,2:T(2,128)(2,1)S(1)}, bf16[2,35,64]{1,0,2:T(2,128)(2,1)}, u32[]{:S(2)}) copy-start(bf16[2,35,64]{1,0,2:T(2,128)(2,1)} %copy-done.76) | copy-start | bytes 26884
  1086.1 52.9 %copy-start.79 = (bf16[2,36,64]{1,0,2:T(2,128)(2,1)S(1)}, bf16[2,36,64]{1,0,2:T(2,128)(2,1)}, u32[]{:S(2)}) copy-start(bf16[2,36,64]{1,0,2:T(2,128)(2,1)} %copy-done.78) | copy-start | bytes 27652
  1086.1 52.9 %copy-start.81 = (bf16[2,37,64]{1,0,2:T(2,128)(2,1)S(1)}, bf16[2,37,64]{1,0,2:T(2,128)(2,1)}, u32[]{:S(2)}) copy-start(bf16[2,37,64]{1,0,2:T(2,128)(2,1)} %copy-done.80) | copy-start | bytes 28420
  (44 other events, 682.2 us)
Sparse Core Ops, SparseCore 0:
  9.4 158.4 all-gather.2
  197.6 109.2 all-reduce.4
  741.0 155.0 all-gather.4
  925.9 109.2 all-reduce.6
where the time goes:
time: 1500 us; the launch traced here: 1480 us
  waiting for transfers between devices  583 us (39%)
  local copies, waits for them, and re-layouts  548 us (37%)
  matrix products  219 us (15%)
  blocking collectives  60 us (4%)
  other arithmetic  40.8 us (3%)
  between operations  16.1 us (1%)
    all_gather x2, waiting for transfers between devices, body(): lax.all_gather(current, 'row', axis=1, tiled=True)  316 us
    unnamed x6, waiting for transfers between devices  218 us
    squeeze x161, local copies, waits for them, and re-layouts, pick_levels(): pieces.append(projected[:, freq_index, skip:, :])  188 us
    unnamed x180, local copies, waits for them, and re-layouts  134 us
    slice x174, local copies, waits for them, and re-layouts, spread_levels(): pieces.append(halves[:, start:start + count, :])  99.9 us
    dot_general x2, matrix products, contrast_apply(): jnp.einsum('cktq,qp->cktp', latitude, fourier, precision=triple, preferre...  79.2 us
    dot_general x2, local copies, waits for them, and re-layouts, contrast_apply(): jnp.einsum('cktp,qp->cktq', weighted, fourier, precision=triple, preferre...  44.3 us
    dot_general x2, matrix products, body(): jnp.dot(tmatrix, lax.all_gather(current, 'row', axis=1, tiled=True), pref...  42.9 us
  transfers between devices with their start and end apart: 6, of which 6 were waited for; matrix products, arithmetic and copies ran while one was open for 0% of the time, Pallas kernels for 0%

commit v1 on v0

--- a/solution.py
+++ b/solution.py
@@ -128,7 +128,15 @@
         summed = lax.psum_scatter(
             grouped.astype(jnp.bfloat16), "col", scatter_dimension=2, tiled=True
         )
-        arrived = lax.all_to_all(summed, "row", split_axis=1, concat_axis=0, tiled=True)
+        ways, here = (lax.axis_size("row"), lax.axis_index("row"))
+        width = summed.shape[1] // ways
+        turned = jnp.roll(summed, -here * width, axis=1)
+        got = [lax.slice_in_dim(turned, 0, width, axis=1)]
+        for far in range(1, ways):
+            sent = lax.slice_in_dim(turned, far * width, (far + 1) * width, axis=1)
+            got.append(lax.ppermute(sent, "row", [(d, (d + far) % ways) for d in range(ways)]))
+        line = jnp.concatenate(got[::-1], axis=0)
+        arrived = jnp.roll(line, (here + 1) * got[0].shape[0], axis=0)
         coupled = contrast_apply(
             arrived.reshape(arrived.shape[0], arrived.shape[3]), contrast, LDEG
         )

time: 1500 us -> 1490 us (level)
  blocking collectives: 60 us -> 20.5 us
  waiting for transfers between devices: 583 us -> 602 us
    ppermute x0 -> x14, waiting for transfers between devices: none -> 51.4 us  [body(): lax.ppermute(sent, 'row', [(d, (d + far) % ways) for d in range(ways)])]
    all_to_all x1 -> x0, blocking collectives: 39.5 us -> none  [body(): lax.all_to_all(summed, 'row', split_axis=1, concat_axis=0, tiled=True)]
    all_to_all x1 -> x0, waiting for transfers between devices: 33.1 us -> none  [body(): lax.all_to_all(summed, 'row', split_axis=1, concat_axis=0, tiled=True)]
    ppermute x0 -> x14, starting transfers between devices: none -> 17.8 us  [body(): lax.ppermute(sent, 'row', [(d, (d + far) % ways) for d in range(ways)])]
    unnamed x180 -> x182, local copies, waits for them, and re-layouts: 134 us -> 133 us
  transfers between devices with their start and end apart: 6 -> 19, of which waited for: 6 -> 13; matrix products, arithmetic and copies ran while one was open for 0% -> 0% of each run, Pallas kernels for 0% -> 0%
where the time goes in v1:
time: 1490 us; the launch traced here: 1470 us
  waiting for transfers between devices  602 us (40%)
  local copies, waits for them, and re-layouts  547 us (37%)
  matrix products  219 us (15%)
  other arithmetic  44.5 us (3%)
  starting transfers between devices  21.5 us (1%)
  blocking collectives  20.5 us (1%)
  between operations  16.2 us (1%)
    all_gather x2, waiting for transfers between devices, body(): lax.all_gather(current, 'row', axis=1, tiled=True)  316 us
    unnamed x6, waiting for transfers between devices  218 us
    squeeze x161, local copies, waits for them, and re-layouts, pick_levels(): pieces.append(projected[:, freq_index, skip:, :])  187 us
    unnamed x182, local copies, waits for them, and re-layouts  133 us
    slice x174, local copies, waits for them, and re-layouts, spread_levels(): pieces.append(halves[:, start:start + count, :])  98.6 us
    dot_general x2, matrix products, contrast_apply(): jnp.einsum('cktq,qp->cktp', latitude, fourier, precision=triple, preferre...  79 us
    ppermute x14, waiting for transfers between devices, body(): lax.ppermute(sent, 'row', [(d, (d + far) % ways) for d in range(ways)])  51.4 us
    dot_general x2, local copies, waits for them, and re-layouts, contrast_apply(): jnp.einsum('cktp,qp->cktq', weighted, fourier, precision=triple, preferre...  44.3 us
  transfers between devices with their start and end apart: 19, of which 13 were waited for; matrix products, arithmetic and copies ran while one was open for 0% of the time, Pallas kernels for 0%

profile of v1, /device:TPU:0, one launch (start us, length us, event | category | flops | bytes accessed | tf_op | source)
XLA Modules:
  0.0 1470.4 jit_solution(16108562361728686554)
XLA Ops:
  7.3 160.5 %all-gather.3.cloned.1.call-done = bf16[2664,2048]{1,0:T(8,128)(2,1)} async-done(((bf16[2664,256]{1,0:T(8,128)(2,1)}), bf16[2664,2048]{1,0:T(8,128)(2,1)}) %all-gather.3.cloned.1.call-update) | async-done | bytes 10911760 | tf_op jit(solution)/shard_map/all_gather | solution.py:124
  167.9 21.5 %convolution_convert_fusion.1 = bf16[1332,2048]{1,0:T(8,128)(2,1)} fusion(bf16[1332,2664]{1,0:T(8,128)(2,1)} %param.15, bf16[2664,2048]{1,0:T(8,128)(2,1)} %all-gather.3.cloned.1.call-done), kind=kOutput, calls=%fused_computation.21 | convolution fusion | flops 14537170944 | bytes 23464512 | tf_op jit(solution)/shard_map/dot_general | solution.py:122
  189.3 8.3 copy.49
  198.9 108.1 %all-reduce.5.cloned.1.call-done = bf16[1332,8,4,64]{0,3,2,1:T(8,128)(2,1)} async-done(((bf16[1332,8,4,64]{0,3,2,1:T(8,128)(2,1)}), bf16[1332,8,4,64]{0,3,2,1:T(8,128)(2,1)}) %all-reduce.5.cloned.1.call-update) | async-done | bytes 5455888
  307.0 2.1 constant_dynamic-slice_fusion.1
  309.9 4.3 collective-permute-start
  314.7 2.9 collective-permute-start.3
  319.6 3.4 collective-permute-done.1
  323.8 3.1 collective-permute-done.2
  326.9 17.8 %collective-permute-done.3 = bf16[1332,1,1,64]{0,3,2,1:T(8,128)(2,1)S(1)} collective-permute-done((bf16[1332,1,1,64]{0,3,2,1:T(8,128)(2,1)S(1)}, bf16[1332,1,1,64]{0,3,2,1:T(8,128)(2,1)S(1)}, u32[]{:S(2)}, u32[]{:S(2)}) %collective-permute-start.3) | collective-permute-done | bytes 170528 | tf_op jit(solution)/shard_map/ppermute | solution.py:137
  345.7 2.4 concatenate.28
  405.3 5.4 concatenate.44
  424.8 55.6 %concatenate.43 = bf16[2,9417,64]{1,0,2:T(2,128)(2,1)} concatenate(bf16[2,144,64]{1,0,2:T(2,128)(2,1)S(1)} %slice.2711, bf16[2,1,64]{1,0,2:T(2,128)(2,1)S(1)} %broadcast.224, bf16[2,71,64]{1,0,2:T(2,128)(2,1)} %get-tuple-element.472, bf16[2,2,64]{1,0,2:T(2,128)(2,1)S(1)} %broadcast.225, bf16[2,70,64]{1,0,2:T(2,128)(2,1)} %get-tuple-element.470, ...), dimensions={1} | concatenate | bytes 4821504
  480.4 4.3 pad_maximum_fusion
  484.7 9.2 reshape.59
  493.9 13.2 convolution_bitcast_fusion.1
  507.1 39.5 %fusion.8 = f32[2,64,144,288]{3,2,1,0:T(8,128)} fusion(f32[145,288,1,1]{1,0,3,2:T(8,128)S(1)} %copy-done.6, f32[2,64,144,145]{2,1,0,3:T(8,128)} %convolution_bitcast_fusion.1), kind=kOutput, calls=%fused_computation.10 | convolution fusion | flops 4618321920 | bytes 32091264 | tf_op jit(solution)/shard_map/cktq,qp->cktp/dot_general | solution.py:95
  546.6 15.1 %multiply_add_fusion.3 = (f32[1,64,144,288]{3,2,1,0:T(8,128)S(1)}, f32[1,64,144,288]{3,2,1,0:T(8,128)}) fusion(f32[2,64,144,288]{3,2,1,0:T(8,128)} %fusion.8, f32[144,288]{1,0:T(8,128)} %get-tuple-element.475, f32[144,288]{1,0:T(8,128)S(1)} %get-tuple-element.473, f32[144,288]{1,0:T(8,128)S(1)} %get-tuple-element.474), kind=kLoop, calls=%fused_computation.17 | loop fusion | flops 15925248 | bytes 42964992 | tf_op jit(solution)/shard_map/add | solution.py:98
  561.7 20.4 %fusion = f32[2,64,144,145]{3,2,1,0:T(8,128)} fusion(f32[145,288,1,1]{1,0,3,2:T(8,128)} %constant.46, f32[1,64,144,288]{3,2,1,0:T(8,128)} %get-tuple-element.10, f32[1,64,144,288]{3,2,1,0:T(8,128)S(1)} %get-tuple-element.9, f32[144]{0:T(256)S(1)} %copy-done.85), kind=kOutput, calls=%fused_computation.1 | convolution fusion | flops 4628938752 | bytes 32091840 | tf_op jit(solution)/shard_map/cktp,qp->cktq/dot_general | solution.py:101
  582.1 22.2 %copy.53 = f32[2,64,144,145]{2,1,0,3:T(8,128)} copy(f32[2,64,144,145]{3,2,1,0:T(8,128)} %fusion) | data formatting | bytes 21381120 | tf_op jit(solution)/shard_map/cktp,qp->cktq/dot_general | solution.py:101
  604.2 15.1 %convert_bitcast_fusion.1 = bf16[2,145,72,64]{2,3,0,1:T(8,128)(2,1)} fusion(f32[2,64,144,145]{2,1,0,3:T(8,128)} %copy.53, f32[145,72,144,1]{2,1,3,0:T(8,128)} %constant.47), kind=kOutput, calls=%fused_computation.26 | convolution fusion | flops 1155916800 | bytes 19376640 | tf_op jit(solution)/shard_map/qlt,cktq->cqlk/dot_general | solution.py:104
  706.2 5.7 concatenate.30
  715.6 3.5 all-to-all-start
  719.2 1.8 copy.48
  721.0 16.0 %all-to-all-done = bf16[4,2664,1,64]{1,3,2,0:T(8,128)(2,1)S(1)} async-done(((bf16[4,2664,1,64]{1,3,2,0:T(8,128)(2,1)}), bf16[4,2664,1,64]{1,3,2,0:T(8,128)(2,1)S(1)}, u32[]{:S(2)}, u32[]{:S(2)}) %all-to-all-start) | async-done | bytes 1364000 | tf_op jit(solution)/shard_map/all_to_all | solution.py:144
  738.7 155.3 %all-gather.5.cloned.1.call-done = bf16[2664,2048]{0,1:T(8,128)(2,1)} async-done(((bf16[2664,256]{0,1:T(8,128)(2,1)}), bf16[2664,2048]{0,1:T(8,128)(2,1)}) %all-gather.5.cloned.1.call-update) | async-done | bytes 10911760 | tf_op jit(solution)/shard_map/all_gather | solution.py:124
  894.0 21.6 %fusion.12 = bf16[1332,2048]{1,0:T(8,128)(2,1)} fusion(bf16[2664,2048]{0,1:T(8,128)(2,1)} %all-gather.5.cloned.1.call-done, bf16[1332,2664]{1,0:T(8,128)(2,1)} %param.15), kind=kOutput, calls=%fused_computation.22 | convolution fusion | flops 14537170944 | bytes 23464512 | tf_op jit(solution)/shard_map/dot_general | solution.py:122
  915.6 8.2 copy.58
  923.8 109.4 %all-reduce.7.cloned.1.call-done = bf16[1332,8,4,64]{0,3,2,1:T(8,128)(2,1)} async-done(((bf16[1332,8,4,64]{0,3,2,1:T(8,128)(2,1)}), bf16[1332,8,4,64]{0,3,2,1:T(8,128)(2,1)}) %all-reduce.7.cloned.1.call-update) | async-done | bytes 5455888
  1033.2 2.1 constant_dynamic-slice_fusion
  1036.0 2.5 collective-permute-start.10
  1038.5 2.4 collective-permute-start.11
  1042.0 3.6 collective-permute-start.7
  1045.6 10.0 collective-permute-done.10
  1055.6 8.6 collective-permute-done.11
  1064.2 6.7 collective-permute-done.9
  1128.7 4.7 concatenate.41
  1133.8 59.3 %concatenate.40 = bf16[2,9417,64]{1,0,2:T(2,128)(2,1)} concatenate(bf16[2,144,64]{1,0,2:T(2,128)(2,1)S(1)} %slice.3009, bf16[2,1,64]{1,0,2:T(2,128)(2,1)S(1)} %copy-done.9, bf16[2,71,64]{1,0,2:T(2,128)(2,1)} %get-tuple-element.360, bf16[2,2,64]{1,0,2:T(2,128)(2,1)S(1)} %copy-done.11, bf16[2,70,64]{1,0,2:T(2,128)(2,1)} %get-tuple-element.358, bf16[2,3,64]{1,0,2:T(2,128)(2,1)S(1)} %copy-done.13, ...), dimensions={1} | concatenate | bytes 4821504
  1193.1 4.3 pad_maximum_fusion.1
  1197.4 9.2 reshape.60
  1206.6 13.2 convolution_bitcast_fusion
  1219.8 39.5 %fusion.6 = f32[2,64,144,288]{3,2,1,0:T(8,128)} fusion(f32[145,288,1,1]{1,0,3,2:T(8,128)S(1)} %copy-done.7, f32[2,64,144,145]{2,1,0,3:T(8,128)} %convolution_bitcast_fusion), kind=kOutput, calls=%fused_computation.8 | convolution fusion | flops 4618321920 | bytes 32091264 | tf_op jit(solution)/shard_map/cktq,qp->cktp/dot_general | solution.py:95
  1259.4 15.1 %multiply_add_fusion.1 = (f32[1,64,144,288]{3,2,1,0:T(8,128)S(1)}, f32[1,64,144,288]{3,2,1,0:T(8,128)}) fusion(f32[2,64,144,288]{3,2,1,0:T(8,128)} %fusion.6, f32[144,288]{1,0:T(8,128)} %get-tuple-element.475, f32[144,288]{1,0:T(8,128)S(1)} %copy-done.3, f32[144,288]{1,0:T(8,128)S(1)} %copy-done.5), kind=kLoop, calls=%fused_computation.13 | loop fusion | flops 15925248 | bytes 42964992 | tf_op jit(solution)/shard_map/add | solution.py:98
  1274.4 20.4 %fusion.3 = f32[2,64,144,145]{3,2,1,0:T(8,128)} fusion(f32[145,288,1,1]{1,0,3,2:T(8,128)} %constant.46, f32[1,64,144,288]{3,2,1,0:T(8,128)} %get-tuple-element.8, f32[1,64,144,288]{3,2,1,0:T(8,128)S(1)} %get-tuple-element.6, f32[144]{0:T(256)S(1)} %copy-done.86), kind=kOutput, calls=%fused_computation.5 | convolution fusion | flops 4628938752 | bytes 32091840 | tf_op jit(solution)/shard_map/cktp,qp->cktq/dot_general | solution.py:101
  1294.8 22.2 %copy.62 = f32[2,64,144,145]{2,1,0,3:T(8,128)} copy(f32[2,64,144,145]{3,2,1,0:T(8,128)} %fusion.3) | data formatting | bytes 21381120 | tf_op jit(solution)/shard_map/cktp,qp->cktq/dot_general | solution.py:101
  1317.0 14.9 %convert_bitcast_fusion = bf16[2,145,72,64]{2,3,0,1:T(8,128)(2,1)} fusion(f32[2,64,144,145]{2,1,0,3:T(8,128)} %copy.62, f32[145,72,144,1]{2,1,3,0:T(8,128)} %constant.47), kind=kOutput, calls=%fused_computation.25 | convolution fusion | flops 1155916800 | bytes 19376640 | tf_op jit(solution)/shard_map/qlt,cktq->cqlk/dot_general | solution.py:104
  1432.7 5.7 concatenate.33
  1440.9 20.5 %all_to_all.8 = bf16[4,2664,1,64]{1,3,2,0:T(8,128)(2,1)S(1)} all-to-all(bf16[4,2664,1,64]{1,3,2,0:T(8,128)(2,1)S(1)} %copy.66), channel_id=1, replica_groups=mesh['row'=8,'col'=4] {'col'}, dimensions={0} | all-to-all | bytes 2727936 | tf_op jit(solution)/shard_map/all_to_all | solution.py:144
  (627 shorter events, 333.5 us)
Async XLA Ops:
  6.5 161.3 %all-gather.3.cloned.1.call-start = ((), (), s32[]{:S(2)}) async-start(), calls=%async_computation.2 | async-start | bytes 12275712 | tf_op jit(solution)/shard_map/all_gather | solution.py:124
  7.3 299.8 %all-reduce.5.cloned.1.call-start = ((), (), s32[]{:S(2)}) async-start(), calls=%async_computation.4 | async-start | bytes 11534336
  197.6 125.4 %copy-start.82 = (f32[3,144,288]{2,1,0:T(8,128)S(1)}, f32[3,144,288]{2,1,0:T(8,128)}, u32[]{:S(2)}) copy-start(f32[3,144,288]{2,1,0:T(8,128)} %param.17) | copy-start | bytes 1492996
  309.9 9.3 collective-permute-start
  314.2 8.9 collective-permute-start.1
  314.7 12.2 collective-permute-start.2
  314.7 30.0 %collective-permute-start.3 = (bf16[1332,1,1,64]{0,3,2,1:T(8,128)(2,1)S(1)}, bf16[1332,1,1,64]{0,3,2,1:T(8,128)(2,1)S(1)}, u32[]{:S(2)}, u32[]{:S(2)}) collective-permute-start(bf16[1332,1,1,64]{0,3,2,1:T(8,128)(2,1)S(1)} %get-tuple-element.245), channel_id=1, source_target_pairs={{0,16},{4,20},{8,24},{12,28},{16,0},{20,4},{24,8},{28,12},{1,17},{... | collective-permute-start | bytes 511496 | tf_op jit(solution)/shard_map/ppermute | solution.py:137
  317.6 27.4 %collective-permute-start.4 = (bf16[1332,1,1,64]{0,3,2,1:T(8,128)(2,1)S(1)}, bf16[1332,1,1,64]{0,3,2,1:T(8,128)(2,1)S(1)}, u32[]{:S(2)}, u32[]{:S(2)}) collective-permute-start(bf16[1332,1,1,64]{0,3,2,1:T(8,128)(2,1)S(1)} %get-tuple-element.244), channel_id=1, source_target_pairs={{0,12},{4,16},{8,20},{12,24},{16,28},{20,0},{24,4},{28,8},{1,13},{... | collective-permute-start | bytes 511496 | tf_op jit(solution)/shard_map/ppermute | solution.py:137
  319.2 25.9 %collective-permute-start.5 = (bf16[1332,1,1,64]{0,3,2,1:T(8,128)(2,1)S(1)}, bf16[1332,1,1,64]{0,3,2,1:T(8,128)(2,1)S(1)}, u32[]{:S(2)}, u32[]{:S(2)}) collective-permute-start(bf16[1332,1,1,64]{0,3,2,1:T(8,128)(2,1)S(1)} %get-tuple-element.243), channel_id=1, source_target_pairs={{0,8},{4,12},{8,16},{12,20},{16,24},{20,28},{24,0},{28,4},{1,9},{5... | collective-permute-start | bytes 511496 | tf_op jit(solution)/shard_map/ppermute | solution.py:137
  323.1 22.0 %collective-permute-start.6 = (bf16[1332,1,1,64]{0,3,2,1:T(8,128)(2,1)S(1)}, bf16[1332,1,1,64]{0,3,2,1:T(8,128)(2,1)S(1)}, u32[]{:S(2)}, u32[]{:S(2)}) collective-permute-start(bf16[1332,1,1,64]{0,3,2,1:T(8,128)(2,1)S(1)} %get-tuple-element.242), channel_id=1, source_target_pairs={{0,4},{4,8},{8,12},{12,16},{16,20},{20,24},{24,28},{28,0},{1,5},{5... | collective-permute-start | bytes 511496 | tf_op jit(solution)/shard_map/ppermute | solution.py:137
  323.8 222.8 %copy-start.2 = (f32[144,288]{1,0:T(8,128)}, f32[144,288]{1,0:T(8,128)S(1)}, u32[]{:S(2)}) copy-start(f32[144,288]{1,0:T(8,128)S(1)} %get-tuple-element.473) | copy-start | bytes 497668
  323.8 222.8 %copy-start.4 = (f32[144,288]{1,0:T(8,128)}, f32[144,288]{1,0:T(8,128)S(1)}, u32[]{:S(2)}) copy-start(f32[144,288]{1,0:T(8,128)S(1)} %get-tuple-element.474) | copy-start | bytes 497668
  410.7 69.7 %copy-start.8 = (bf16[2,1,64]{1,0,2:T(2,128)(2,1)}, bf16[2,1,64]{1,0,2:T(2,128)(2,1)S(1)}, u32[]{:S(2)}) copy-start(bf16[2,1,64]{1,0,2:T(2,128)(2,1)S(1)} %broadcast.224) | copy-start | bytes 772
  410.7 69.7 %copy-start.10 = (bf16[2,2,64]{1,0,2:T(2,128)(2,1)}, bf16[2,2,64]{1,0,2:T(2,128)(2,1)S(1)}, u32[]{:S(2)}) copy-start(bf16[2,2,64]{1,0,2:T(2,128)(2,1)S(1)} %broadcast.225) | copy-start | bytes 1540
  410.8 69.6 %copy-start.12 = (bf16[2,3,64]{1,0,2:T(2,128)(2,1)}, bf16[2,3,64]{1,0,2:T(2,128)(2,1)S(1)}, u32[]{:S(2)}) copy-start(bf16[2,3,64]{1,0,2:T(2,128)(2,1)S(1)} %broadcast.226) | copy-start | bytes 2308
  715.6 21.5 %all-to-all-start = ((bf16[4,2664,1,64]{1,3,2,0:T(8,128)(2,1)}), bf16[4,2664,1,64]{1,3,2,0:T(8,128)(2,1)S(1)}, u32[]{:S(2)}, u32[]{:S(2)}) async-start(bf16[4,2664,1,64]{1,3,2,0:T(8,128)(2,1)} %copy.57), calls=%async_computation | async-start | bytes 2752512 | tf_op jit(solution)/shard_map/all_to_all | solution.py:144
  719.1 174.9 %all-gather.5.cloned.1.call-start = ((), (), s32[]{:S(2)}) async-start(), calls=%async_computation.3 | async-start | bytes 12386304 | tf_op jit(solution)/shard_map/all_gather | solution.py:124
  738.6 294.5 %all-reduce.7.cloned.1.call-start = ((), (), s32[]{:S(2)}) async-start(), calls=%async_computation.5 | async-start | bytes 11534336
  1036.0 19.5 %collective-permute-start.10 = (bf16[1332,1,1,64]{0,3,2,1:T(8,128)(2,1)S(1)}, bf16[1332,1,1,64]{0,3,2,1:T(8,128)(2,1)S(1)}, u32[]{:S(2)}, u32[]{:S(2)}) collective-permute-start(bf16[1332,1,1,64]{0,3,2,1:T(8,128)(2,1)S(1)} %get-tuple-element.237), channel_id=1, source_target_pairs={{0,16},{4,20},{8,24},{12,28},{16,0},{20,4},{24,8},{28,12},{1,17},{... | collective-permute-start | bytes 511496 | tf_op jit(solution)/shard_map/ppermute | solution.py:137
  1038.5 25.6 %collective-permute-start.11 = (bf16[1332,1,1,64]{0,3,2,1:T(8,128)(2,1)S(1)}, bf16[1332,1,1,64]{0,3,2,1:T(8,128)(2,1)S(1)}, u32[]{:S(2)}, u32[]{:S(2)}) collective-permute-start(bf16[1332,1,1,64]{0,3,2,1:T(8,128)(2,1)S(1)} %get-tuple-element.236), channel_id=1, source_target_pairs={{0,12},{4,16},{8,20},{12,24},{16,28},{20,0},{24,4},{28,8},{1,13},{... | collective-permute-start | bytes 511496 | tf_op jit(solution)/shard_map/ppermute | solution.py:137
  1040.9 23.3 %collective-permute-start.12 = (bf16[1332,1,1,64]{0,3,2,1:T(8,128)(2,1)S(1)}, bf16[1332,1,1,64]{0,3,2,1:T(8,128)(2,1)S(1)}, u32[]{:S(2)}, u32[]{:S(2)}) collective-permute-start(bf16[1332,1,1,64]{0,3,2,1:T(8,128)(2,1)S(1)} %get-tuple-element.235), channel_id=1, source_target_pairs={{0,8},{4,12},{8,16},{12,20},{16,24},{20,28},{24,0},{28,4},{1,9},{5... | collective-permute-start | bytes 511496 | tf_op jit(solution)/shard_map/ppermute | solution.py:137
  1040.9 23.3 %collective-permute-start.13 = (bf16[1332,1,1,64]{0,3,2,1:T(8,128)(2,1)S(1)}, bf16[1332,1,1,64]{0,3,2,1:T(8,128)(2,1)S(1)}, u32[]{:S(2)}, u32[]{:S(2)}) collective-permute-start(bf16[1332,1,1,64]{0,3,2,1:T(8,128)(2,1)S(1)} %get-tuple-element.234), channel_id=1, source_target_pairs={{0,4},{4,8},{8,12},{12,16},{16,20},{20,24},{24,28},{28,0},{1,5},{5... | collective-permute-start | bytes 511496 | tf_op jit(solution)/shard_map/ppermute | solution.py:137
  1042.0 22.2 %collective-permute-start.7 = (bf16[1332,1,1,64]{0,3,2,1:T(8,128)(2,1)S(1)}, bf16[1332,1,1,64]{0,3,2,1:T(8,128)(2,1)S(1)}, u32[]{:S(2)}, u32[]{:S(2)}) collective-permute-start(bf16[1332,1,1,64]{0,3,2,1:T(8,128)(2,1)S(1)} %get-tuple-element.240), channel_id=1, source_target_pairs={{0,28},{4,0},{8,4},{12,8},{16,12},{20,16},{24,20},{28,24},{1,29},{... | collective-permute-start | bytes 511496 | tf_op jit(solution)/shard_map/ppermute | solution.py:137
  1055.6 8.6 collective-permute-start.8
  1064.1 6.7 collective-permute-start.9
  1081.2 52.3 %copy-start.17 = (bf16[2,5,64]{1,0,2:T(2,128)(2,1)S(1)}, bf16[2,5,64]{1,0,2:T(2,128)(2,1)}, u32[]{:S(2)}) copy-start(bf16[2,5,64]{1,0,2:T(2,128)(2,1)} %copy-done.16) | copy-start | bytes 3844
  1081.2 52.3 %copy-start.19 = (bf16[2,6,64]{1,0,2:T(2,128)(2,1)S(1)}, bf16[2,6,64]{1,0,2:T(2,128)(2,1)}, u32[]{:S(2)}) copy-start(bf16[2,6,64]{1,0,2:T(2,128)(2,1)} %copy-done.18) | copy-start | bytes 4612
  1081.2 52.3 %copy-start.21 = (bf16[2,7,64]{1,0,2:T(2,128)(2,1)S(1)}, bf16[2,7,64]{1,0,2:T(2,128)(2,1)}, u32[]{:S(2)}) copy-start(bf16[2,7,64]{1,0,2:T(2,128)(2,1)} %copy-done.20) | copy-start | bytes 5380
  1081.2 52.3 %copy-start.23 = (bf16[2,8,64]{1,0,2:T(2,128)(2,1)S(1)}, bf16[2,8,64]{1,0,2:T(2,128)(2,1)}, u32[]{:S(2)}) copy-start(bf16[2,8,64]{1,0,2:T(2,128)(2,1)} %copy-done.22) | copy-start | bytes 6148
  1081.2 52.3 %copy-start.25 = (bf16[2,9,64]{1,0,2:T(2,128)(2,1)S(1)}, bf16[2,9,64]{1,0,2:T(2,128)(2,1)}, u32[]{:S(2)}) copy-start(bf16[2,9,64]{1,0,2:T(2,128)(2,1)} %copy-done.24) | copy-start | bytes 6916
  1081.2 52.3 %copy-start.27 = (bf16[2,10,64]{1,0,2:T(2,128)(2,1)S(1)}, bf16[2,10,64]{1,0,2:T(2,128)(2,1)}, u32[]{:S(2)}) copy-start(bf16[2,10,64]{1,0,2:T(2,128)(2,1)} %copy-done.26) | copy-start | bytes 7684
  1081.3 52.3 %copy-start.29 = (bf16[2,11,64]{1,0,2:T(2,128)(2,1)S(1)}, bf16[2,11,64]{1,0,2:T(2,128)(2,1)}, u32[]{:S(2)}) copy-start(bf16[2,11,64]{1,0,2:T(2,128)(2,1)} %copy-done.28) | copy-start | bytes 8452
  1081.3 52.3 %copy-start.31 = (bf16[2,12,64]{1,0,2:T(2,128)(2,1)S(1)}, bf16[2,12,64]{1,0,2:T(2,128)(2,1)}, u32[]{:S(2)}) copy-start(bf16[2,12,64]{1,0,2:T(2,128)(2,1)} %copy-done.30) | copy-start | bytes 9220
  1081.3 52.3 %copy-start.33 = (bf16[2,13,64]{1,0,2:T(2,128)(2,1)S(1)}, bf16[2,13,64]{1,0,2:T(2,128)(2,1)}, u32[]{:S(2)}) copy-start(bf16[2,13,64]{1,0,2:T(2,128)(2,1)} %copy-done.32) | copy-start | bytes 9988
  1081.3 52.3 %copy-start.35 = (bf16[2,14,64]{1,0,2:T(2,128)(2,1)S(1)}, bf16[2,14,64]{1,0,2:T(2,128)(2,1)}, u32[]{:S(2)}) copy-start(bf16[2,14,64]{1,0,2:T(2,128)(2,1)} %copy-done.34) | copy-start | bytes 10756
  1081.3 52.3 %copy-start.37 = (bf16[2,15,64]{1,0,2:T(2,128)(2,1)S(1)}, bf16[2,15,64]{1,0,2:T(2,128)(2,1)}, u32[]{:S(2)}) copy-start(bf16[2,15,64]{1,0,2:T(2,128)(2,1)} %copy-done.36) | copy-start | bytes 11524
  1081.3 52.3 %copy-start.39 = (bf16[2,16,64]{1,0,2:T(2,128)(2,1)S(1)}, bf16[2,16,64]{1,0,2:T(2,128)(2,1)}, u32[]{:S(2)}) copy-start(bf16[2,16,64]{1,0,2:T(2,128)(2,1)} %copy-done.38) | copy-start | bytes 12292
  1081.3 52.3 %copy-start.41 = (bf16[2,17,64]{1,0,2:T(2,128)(2,1)S(1)}, bf16[2,17,64]{1,0,2:T(2,128)(2,1)}, u32[]{:S(2)}) copy-start(bf16[2,17,64]{1,0,2:T(2,128)(2,1)} %copy-done.40) | copy-start | bytes 13060
  1081.3 52.3 %copy-start.43 = (bf16[2,18,64]{1,0,2:T(2,128)(2,1)S(1)}, bf16[2,18,64]{1,0,2:T(2,128)(2,1)}, u32[]{:S(2)}) copy-start(bf16[2,18,64]{1,0,2:T(2,128)(2,1)} %copy-done.42) | copy-start | bytes 13828
  1081.3 52.3 %copy-start.45 = (bf16[2,19,64]{1,0,2:T(2,128)(2,1)S(1)}, bf16[2,19,64]{1,0,2:T(2,128)(2,1)}, u32[]{:S(2)}) copy-start(bf16[2,19,64]{1,0,2:T(2,128)(2,1)} %copy-done.44) | copy-start | bytes 14596
  1081.3 52.3 %copy-start.47 = (bf16[2,20,64]{1,0,2:T(2,128)(2,1)S(1)}, bf16[2,20,64]{1,0,2:T(2,128)(2,1)}, u32[]{:S(2)}) copy-start(bf16[2,20,64]{1,0,2:T(2,128)(2,1)} %copy-done.46) | copy-start | bytes 15364
  1081.4 52.3 %copy-start.49 = (bf16[2,21,64]{1,0,2:T(2,128)(2,1)S(1)}, bf16[2,21,64]{1,0,2:T(2,128)(2,1)}, u32[]{:S(2)}) copy-start(bf16[2,21,64]{1,0,2:T(2,128)(2,1)} %copy-done.48) | copy-start | bytes 16132
  1081.4 52.3 %copy-start.51 = (bf16[2,22,64]{1,0,2:T(2,128)(2,1)S(1)}, bf16[2,22,64]{1,0,2:T(2,128)(2,1)}, u32[]{:S(2)}) copy-start(bf16[2,22,64]{1,0,2:T(2,128)(2,1)} %copy-done.50) | copy-start | bytes 16900
  1081.4 52.3 %copy-start.53 = (bf16[2,23,64]{1,0,2:T(2,128)(2,1)S(1)}, bf16[2,23,64]{1,0,2:T(2,128)(2,1)}, u32[]{:S(2)}) copy-start(bf16[2,23,64]{1,0,2:T(2,128)(2,1)} %copy-done.52) | copy-start | bytes 17668
  1081.4 52.3 %copy-start.55 = (bf16[2,24,64]{1,0,2:T(2,128)(2,1)S(1)}, bf16[2,24,64]{1,0,2:T(2,128)(2,1)}, u32[]{:S(2)}) copy-start(bf16[2,24,64]{1,0,2:T(2,128)(2,1)} %copy-done.54) | copy-start | bytes 18436
  1081.4 52.3 %copy-start.57 = (bf16[2,25,64]{1,0,2:T(2,128)(2,1)S(1)}, bf16[2,25,64]{1,0,2:T(2,128)(2,1)}, u32[]{:S(2)}) copy-start(bf16[2,25,64]{1,0,2:T(2,128)(2,1)} %copy-done.56) | copy-start | bytes 19204
  1081.4 52.3 %copy-start.59 = (bf16[2,26,64]{1,0,2:T(2,128)(2,1)S(1)}, bf16[2,26,64]{1,0,2:T(2,128)(2,1)}, u32[]{:S(2)}) copy-start(bf16[2,26,64]{1,0,2:T(2,128)(2,1)} %copy-done.58) | copy-start | bytes 19972
  1081.4 52.3 %copy-start.61 = (bf16[2,27,64]{1,0,2:T(2,128)(2,1)S(1)}, bf16[2,27,64]{1,0,2:T(2,128)(2,1)}, u32[]{:S(2)}) copy-start(bf16[2,27,64]{1,0,2:T(2,128)(2,1)} %copy-done.60) | copy-start | bytes 20740
  (58 other events, 1354.9 us)
Sparse Core Ops, SparseCore 0:
  9.4 158.4 all-gather.2
  197.7 109.2 all-reduce.4
  738.7 155.2 all-gather.4
  923.9 109.2 all-reduce.6
